TPU v7x, 32 devices: a whole 2x2x4 slice. The times are simulated.
32 devices in a mesh: grp: 2 (over y), ep: 8 (over z, x), seq: 1, rep: 2 (over core).
Axes of the slice: x: 2, y: 2, z: 4, core: 2. Of those that a mesh axis runs over, the one named last changes fastest.
Arguments:
- hidden_in: bfloat16 [1024, 2048], P(('grp', 'ep', 'rep'), 'seq'), parts along dimension 0, may hold values from -64 to 64
- row_counts: int32 [32], P(('grp', 'ep', 'rep')), parts along dimension 0, may hold values from 24 to 32, as said below
- qkv_new: bfloat16 [1024, 3, 2048], P(('grp', 'ep', 'rep')), parts along dimension 0, may hold values from -6 to 6
- cache_len: int32 [16, 64], P('grp', ('rep', 'seq')), parts along dimension 0, may hold values from 1 to 128, as said below
- kv_cache: bfloat16 [2, 16, 64, 128, 2048], P(None, 'grp', ('rep', 'seq'), None, 'ep'), parts along dimension 1, may hold values from -128 to 128
- w_out: bfloat16 [2048, 2048], P('ep', 'seq'), may hold values from -0.125 to 0.125
- moe_gain: float32 [2048], replicated, may hold values from 0.1 to 1.9
- w_in: bfloat16 [16, 2048, 2, 1408], P(('ep', 'rep'), None, None, 'seq'), may hold values from -0.125 to 0.125
- w_down: bfloat16 [16, 1408, 2048], P(('ep', 'rep'), 'seq'), may hold values from -0.15625 to 0.15625
- route_ids: int32 [1024, 6], P(('grp', 'ep', 'rep')), parts along dimension 0, may hold values from 0 to 15, all different within a row; in each aligned block of 32 rows (0 to 31, 32 to 63, ...) at most 24 rows name the same one
- route_weight: bfloat16 [1024, 6], P(('grp', 'ep', 'rep')), parts along dimension 0, may hold values from 0.049804688 to 0.44921875
Outputs:
- mixed: bfloat16 [1024, 2048], P(('grp', 'ep', 'rep'), 'seq'), parts along dimension 0
There are 2 independent parts, one for each index of `grp`. A program takes and returns all parts, laid end to end along the dimension named above; an argument that names none is the same for every part. Nothing has to cross between parts.
Inputs may be any that keep to these rules, and one draw needn't show every extreme that they name: The first row_counts[b] slots of block b are live; some block is full. `cache_len`: some row has 128 cached positions. `route_ids`: a row's 6 experts differ; among the 32 rows of one block no expert is named by more than 24 rows, and in some block one is named by exactly 24.
All inputs are finite; a program needn't handle non-finite values.
Results may differ from a plain program's by a relative error of at most 0.0053.
Values may be sent and summed in bfloat16 or wider, within the bound.
A program may use at most 192 MiB of HBM per device.

v0:
```python
import functools
import math

import jax
import jax.numpy as jnp
from jax import lax
from jax.experimental import pallas as pl
from jax.experimental.pallas import tpu as pltpu
from jax.sharding import PartitionSpec as P

D = 2048
HEAD_DIM = 128
TOPK = 6


epsilon = 1e-06
masked_score = -1e30


def local(
    hidden_in,
    row_counts,
    qkv_new,
    cache_len,
    kv_cache,
    w_out,
    moe_gain,
    w_in,
    w_down,
    route_ids,
    route_weight,
):
    tok_rows, feat_local = hidden_in.shape
    owners = lax.axis_size("ep")
    parts_seq = lax.axis_size("seq")
    width_local = kv_cache.shape[-1]
    heads_local = width_local // HEAD_DIM
    positions = kv_cache.shape[3]
    share_rows = tok_rows // parts_seq
    attend_rows = owners * share_rows
    moved_block = lax.all_to_all(qkv_new, "ep", split_axis=2, concat_axis=0, tiled=True)
    moved_block = moved_block.reshape(owners, tok_rows, 3, width_local)
    heads_block = lax.dynamic_slice_in_dim(
        moved_block, lax.axis_index("seq") * share_rows, share_rows, 1
    )
    heads_block = heads_block.reshape(attend_rows, 3, heads_local, HEAD_DIM)
    queries = heads_block[:, 0]
    key_new = heads_block[:, 1].astype(jnp.float32)
    value_new = heads_block[:, 2].astype(jnp.float32)
    lengths = cache_len.reshape(attend_rows)
    cache_keys = kv_cache[0].reshape(attend_rows, positions, heads_local, HEAD_DIM)
    cache_values = kv_cache[1].reshape(attend_rows, positions, heads_local, HEAD_DIM)
    score_scale = 1.0 / math.sqrt(HEAD_DIM)
    position = jnp.arange(positions, dtype=jnp.int32)
    in_cache = position[None, None, :] < lengths[:, None, None]
    scores = (
        jnp.einsum("nhd,nphd->nhp", queries, cache_keys, preferred_element_type=jnp.float32)
        * score_scale
    )
    scores = jnp.where(in_cache, scores, masked_score)
    own_score = jnp.sum(queries.astype(jnp.float32) * key_new, axis=2) * score_scale
    highest = jnp.maximum(jnp.max(scores, axis=2), own_score)
    weights = jnp.where(in_cache, jnp.exp(scores - highest[..., None]), 0.0)
    partial_sum = jnp.einsum(
        "nhp,nphd->nhd",
        weights.astype(jnp.bfloat16),
        cache_values,
        preferred_element_type=jnp.float32,
    )
    own_weight = jnp.exp(own_score - highest)
    attended = (partial_sum + own_weight[..., None] * value_new) / (
        jnp.sum(weights, axis=2) + own_weight
    )[..., None]
    attended = attended.astype(jnp.bfloat16).reshape(owners, share_rows, width_local)
    attended = lax.all_gather(attended, "seq", axis=1, tiled=True).reshape(
        owners * tok_rows, width_local
    )
    attn_out = lax.psum_scatter(
        jnp.dot(attended, w_out, preferred_element_type=jnp.float32),
        "ep",
        scatter_dimension=0,
        tiled=True,
    )
    residual = (hidden_in.astype(jnp.float32) + attn_out).astype(jnp.bfloat16)
    residual_wide = lax.optimization_barrier(residual).astype(jnp.float32)
    is_live = jnp.arange(tok_rows, dtype=jnp.int32) < row_counts[0]
    expert_total = lax.axis_size(("ep", "rep")) * w_in.shape[0]
    capacity = min(tok_rows, max(2, 2 * tok_rows * TOPK // expert_total))
    pair_count = tok_rows * TOPK
    flat_ids = route_ids.reshape(pair_count)
    pair_hits = (
        flat_ids[:, None] == jnp.arange(expert_total, dtype=jnp.int32)[None, :]
    ) & jnp.repeat(is_live, TOPK)[:, None]
    hit_counts = pair_hits.astype(jnp.int32)
    earlier_hits = jnp.cumsum(hit_counts, axis=0) - hit_counts
    slot_index = jnp.sum(earlier_hits * hit_counts, axis=1)
    target_cell = jnp.where(
        jnp.any(pair_hits, axis=1), flat_ids * capacity + slot_index, -1
    ).reshape(tok_rows, TOPK)
    cell_index = jnp.arange(expert_total * capacity, dtype=jnp.int32)
    cell_hits = target_cell[None, :, :] == cell_index[:, None, None]
    dispatch_rows = jnp.any(cell_hits, axis=2).astype(jnp.bfloat16)
    combine_rows = jnp.sum(
        jnp.where(cell_hits, route_weight.astype(jnp.float32)[None], 0.0), axis=2
    ).astype(jnp.bfloat16)
    full_rows = lax.all_gather(residual, "seq", axis=1, tiled=True)
    rows_wide = full_rows.astype(jnp.float32)
    inverse_rms = lax.rsqrt(jnp.mean(rows_wide * rows_wide, axis=1) + epsilon)
    normed = (rows_wide * inverse_rms[:, None] * moe_gain).astype(jnp.bfloat16)
    outgoing = jnp.dot(dispatch_rows, normed, preferred_element_type=jnp.float32).astype(
        jnp.bfloat16
    )
    outgoing = outgoing.reshape(expert_total, capacity, D)
    arrived = lax.all_to_all(outgoing, ("ep", "rep"), split_axis=0, concat_axis=0, tiled=True)
    sources, slot_count, feature_count = arrived.shape
    flat_rows = arrived.reshape(sources * slot_count, D)
    gate_up = jnp.dot(flat_rows, w_in.reshape(D, -1), preferred_element_type=jnp.float32).reshape(
        sources * slot_count, 2, -1
    )
    hidden_units = (jax.nn.silu(gate_up[:, 0]) * gate_up[:, 1]).astype(jnp.bfloat16)
    down_part = jnp.dot(
        hidden_units, w_down.reshape(-1, D), preferred_element_type=jnp.float32
    ).reshape(sources, slot_count, D)
    summed = lax.psum_scatter(down_part, "seq", scatter_dimension=2, tiled=True).astype(
        jnp.bfloat16
    )
    returned = lax.all_to_all(summed, ("ep", "rep"), split_axis=0, concat_axis=0, tiled=True)
    returned = returned.reshape(expert_total * capacity, feat_local)
    moe_out = lax.dot_general(
        combine_rows, returned, (((0,), (0,)), ((), ())), preferred_element_type=jnp.float32
    )
    mixed = jnp.where(is_live[:, None], residual_wide + moe_out, 0.0).astype(jnp.bfloat16)
    return mixed


LANES = 128
F32 = jnp.float32
BF16 = jnp.bfloat16


def layer_kernel(
    owners,
    qkv_ref,
    lens_ref,
    kv_hbm,
    w_out_ref,
    hidden_ref,
    gain_ref,
    ids_ref,
    gate_ref,
    count_ref,
    w_in_hbm,
    w_down_hbm,
    out_ref,
    kv_buf,
    q_buf,
    pair_out,
    pair_in,
    col_out,
    col_in,
    total,
    rows_all,
    w_in_buf,
    w_down_buf,
    hidden_buf,
    y_all,
    y_in,
    pair_out2,
    pair_in2,
    col_out2,
    col_in2,
    kv_sem,
    w_sem,
    q_send,
    q_recv,
    pair_send,
    pair_recv,
    col_send,
    col_recv,
    z_send,
    x_send,
    s_send,
    g_recv,
    y_send,
    y_recv,
    pair_send2,
    pair_recv2,
    col_send2,
    col_recv2,
):
    cols = owners // 2
    me = lax.axis_index("ep")
    rep = lax.axis_index("rep")
    mz, mx = me // 2, me % 2
    across = mz * 2 + (1 - mx)
    sister = 1 - rep
    block, width = hidden_ref.shape
    part = kv_buf.shape[-1]
    positions = kv_buf.shape[-2]
    heads = part // HEAD_DIM
    used = heads * block

    def remote(src, dst, send, recv, ep=None, core=None):
        return pltpu.make_async_remote_copy(
            src_ref=src,
            dst_ref=dst,
            send_sem=send,
            recv_sem=recv,
            device_id={"ep": me if ep is None else ep, "rep": rep if core is None else core},
            device_id_type=pl.DeviceIdType.MESH,
        )

    def kv_copy(owner, slot):
        return pltpu.make_async_copy(kv_hbm.at[:, owner], kv_buf.at[slot], kv_sem.at[slot])

    def owner_of(j, s):
        z = (mz + 1 + j) % cols
        return z * 2 + (1 - mx if s == 0 else mx)

    in_copy = pltpu.make_async_copy(w_in_hbm, w_in_buf, w_sem.at[0])
    down_copy = pltpu.make_async_copy(w_down_hbm, w_down_buf, w_sem.at[1])
    kv_copy(owner_of(0, 0), 0).start()
    kv_copy(owner_of(0, 1), 1).start()
    in_copy.start()
    down_copy.start()

    barrier = pltpu.get_barrier_semaphore()
    for i in range(1, owners):
        pl.semaphore_signal(
            barrier,
            inc=1,
            device_id={"ep": (me + i) % owners, "rep": rep},
            device_id_type=pl.DeviceIdType.MESH,
        )
    pl.semaphore_signal(
        barrier, inc=1, device_id={"ep": me, "rep": sister}, device_id_type=pl.DeviceIdType.MESH
    )
    pl.semaphore_wait(barrier, owners)

    def q_part(owner):
        return qkv_ref.at[:, :, pl.ds(pl.multiple_of(owner * part, part), part)]

    @pl.loop(1, owners)
    def _(i):
        to = (me + owners - i) % owners
        remote(q_part(to), q_buf.at[me], q_send.at[to], q_recv.at[me], ep=to).start()

    q_buf[me] = qkv_ref[:, :, pl.ds(pl.multiple_of(me * part, part), part)]

    is_live = lax.broadcasted_iota(jnp.int32, (block, 1), 0) < count_ref[0]
    expert_id = lax.broadcasted_iota(jnp.int32, (LANES, LANES), 0)
    gates = gate_ref[...].astype(F32)
    ids = jnp.concatenate([ids_ref[...]] * (LANES // block), axis=1)
    gates = jnp.concatenate([gates] * (LANES // block), axis=1)
    coef = jnp.zeros((LANES, LANES), F32)
    for k in range(TOPK):
        coef += jnp.where(expert_id == ids[k : k + 1], gates[k : k + 1], 0.0)
    coef = coef.T[:block]
    rows_all[mx, rep, mz, :, width:] = jnp.where(is_live, coef, 0.0).astype(BF16)

    lane_row = lax.broadcasted_iota(jnp.int32, (1, LANES), 1) % block
    pos_of = lax.broadcasted_iota(jnp.int32, (positions, LANES), 0)
    head_of = lax.broadcasted_iota(jnp.int32, (block, part), 1) // HEAD_DIM
    row_mod = lax.broadcasted_iota(jnp.int32, (used, positions), 0) % block
    scale = 1.0 / math.sqrt(HEAD_DIM)
    group = 8

    def partial(owner, slot):
        query = q_buf[owner, 0]
        fresh_k = q_buf[owner, 1]
        fresh_v = q_buf[owner, 2].astype(F32)
        zero = jnp.zeros_like(query)
        stack = [jnp.where(head_of == h, query, zero) for h in range(heads)]
        stack += [zero] * (LANES // block - heads)
        queries = jnp.concatenate(stack, axis=0)
        nt = (((1,), (1,)), ((), ()))

        def score_step(g, acc):
            keys = kv_buf[slot, 0, pl.ds(g * group, group)].reshape(group * positions, part)
            got = lax.dot_general(keys, queries, nt, preferred_element_type=F32)
            for r in range(group):
                acc = jnp.where(
                    lane_row == g * group + r, got[r * positions : (r + 1) * positions], acc
                )
            return acc

        scores = lax.fori_loop(
            0, block // group, score_step, jnp.zeros((positions, LANES), F32)
        )
        fresh = lax.dot_general(fresh_k, queries, nt, preferred_element_type=F32)
        diag = lax.broadcasted_iota(jnp.int32, (block, LANES), 0) == (
            lax.broadcasted_iota(jnp.int32, (block, LANES), 1) % block
        )
        own = jnp.sum(jnp.where(diag, fresh, 0.0), axis=0, keepdims=True) * scale
        lens = jnp.concatenate([lens_ref[pl.ds(owner, 1), :]] * (LANES // block), axis=1)
        in_cache = pos_of < lens
        scores = jnp.where(in_cache, scores * scale, masked_score)
        top = jnp.maximum(jnp.max(scores, axis=0, keepdims=True), own)
        weights = jnp.where(in_cache, jnp.exp(scores - top), 0.0)
        own_w = jnp.exp(own - top)
        den = jnp.sum(weights, axis=0, keepdims=True) + own_w
        own_t = jnp.broadcast_to(own_w, (LANES, LANES)).T
        den_t = jnp.broadcast_to(den, (LANES, LANES)).T
        weights_t = weights.T[:used]

        def value_step(g, acc):
            wide = jnp.concatenate(
                [
                    jnp.where(row_mod == g * group + r, weights_t, 0.0).astype(BF16)
                    for r in range(group)
                ],
                axis=1,
            )
            values = kv_buf[slot, 1, pl.ds(g * group, group)].reshape(group * positions, part)
            return acc + jnp.dot(wide, values, preferred_element_type=F32)

        summed = lax.fori_loop(0, block // group, value_step, jnp.zeros((used, part), F32))
        pieces = []
        for h in range(heads):
            rows = slice(h * block, (h + 1) * block)
            lanes = slice(h * HEAD_DIM, (h + 1) * HEAD_DIM)
            pieces.append((summed[rows, lanes] + own_t[rows] * fresh_v[:, lanes]) / den_t[rows])
        attended = jnp.concatenate(pieces, axis=1).astype(BF16)
        return jnp.dot(attended, w_out_ref[...], preferred_element_type=F32)

    def arrive_q(owner):
        @pl.when(owner != me)
        def _():
            remote(q_part(owner), q_buf.at[owner], q_send.at[owner], q_recv.at[owner], ep=owner).wait_recv()

    def pair_copy(z):
        return remote(pair_out.at[z], pair_in.at[z], pair_send.at[z], pair_recv.at[z], ep=across)

    def col_copy(z, slot):
        return remote(
            col_out.at[z], col_in.at[slot], col_send.at[z], col_recv.at[slot], ep=z * 2 + mx
        )

    @pl.loop(0, cols)
    def _(j):
        z = (mz + 1 + j) % cols
        first, second = owner_of(j, 0), owner_of(j, 1)
        arrive_q(first)
        kv_copy(first, 0).wait()
        pair_out[z] = partial(first, 0).astype(BF16)
        pair_copy(z).start()

        @pl.when(j < cols - 1)
        def _():
            kv_copy(owner_of(j + 1, 0), 0).start()

        arrive_q(second)
        kv_copy(second, 1).wait()
        mine = partial(second, 1)

        @pl.when(j < cols - 1)
        def _():
            kv_copy(owner_of(j + 1, 1), 1).start()

        pair_copy(z).wait_recv()
        mine = mine + pair_in[z].astype(F32)

        @pl.when(j < cols - 1)
        def _():
            col_out[z] = mine.astype(BF16)
            col_copy(z, mz).start()

        @pl.when(j == cols - 1)
        def _():
            total[...] = mine

    for j in range(1, cols):
        z = (mz + j) % cols
        col_copy(z, z).wait_recv()
        total[...] += col_in[z].astype(F32)
    residual = (hidden_ref[...].astype(F32) + total[...]).astype(BF16)
    wide = residual.astype(F32)
    total[...] = wide
    inverse = lax.rsqrt(jnp.mean(wide * wide, axis=1, keepdims=True) + epsilon)
    rows_all[mx, rep, mz, :, :width] = (wide * inverse * gain_ref[...]).astype(BF16)

    def row_copy(e, side, send, ep=None, core=None):
        at = rows_all.at[e % 2, side, e // 2]
        return remote(at, at, send, g_recv.at[e % 2, side, e // 2], ep=ep, core=core)

    def z_copy(z, e):
        return row_copy(e, rep, z_send.at[z], ep=z * 2 + mx)

    def x_copy(e):
        return row_copy(e, rep, x_send.at[e], ep=across)

    def s_copy(e, side):
        return row_copy(e, side, s_send.at[e], core=sister)

    def y_copy(x):
        return remote(y_all.at[x, sister], y_in.at[x], y_send.at[x], y_recv.at[x], core=sister)

    expert = me * 2 + rep
    tiles = w_in_buf.shape[2] // LANES
    half = owners * block
    step = 2 * LANES

    def experts(x):
        @pl.loop(0, tiles)
        def _(n):
            rows = rows_all[x, :, :, :, :width].reshape(half, width)
            lanes = pl.ds(pl.multiple_of(n * LANES, LANES), LANES)
            both_w = jnp.concatenate([w_in_buf[0, :, lanes], w_in_buf[1, :, lanes]], axis=1)
            both = jnp.dot(rows, both_w, preferred_element_type=F32)
            gate, up = both[:, :LANES], both[:, LANES:]
            hidden_buf[:, lanes] = (gate / (1.0 + jnp.exp(-gate)) * up).astype(BF16)

        coefs = rows_all[x, :, :, :, width:].reshape(half, LANES).astype(F32)
        lane = lax.broadcasted_iota(jnp.int32, (half, LANES), 1)
        factor = jnp.sum(jnp.where(lane == expert, coefs, 0.0), axis=1, keepdims=True)

        @pl.loop(0, width // step)
        def _(n):
            lanes = pl.ds(pl.multiple_of(n * step, step), step)
            made = jnp.dot(hidden_buf[...], w_down_buf[:, lanes], preferred_element_type=F32)
            made = made.astype(BF16).astype(F32) * factor
            y_all[x, :, :, :, lanes] = made.astype(BF16).reshape(2, cols, block, step)

    for j in range(1, cols):
        z_copy((mz + j) % cols, me).start()
    x_copy(me).start()
    s_copy(me, rep).start()
    for j in range(1, cols):
        e = ((mz + j) % cols) * 2 + mx
        z_copy(e // 2, e).wait_recv()
        x_copy(e).start()
        s_copy(e, rep).start()
    in_copy.wait()
    down_copy.wait()
    for z in range(cols):
        s_copy(z * 2 + mx, sister).wait_recv()
    experts(mx)
    y_copy(mx).start()
    for j in range(cols):
        e = ((mz + j) % cols) * 2 + 1 - mx
        x_copy(e).wait_recv()
        s_copy(e, rep).start()
    for z in range(cols):
        s_copy(z * 2 + 1 - mx, sister).wait_recv()
    experts(1 - mx)
    y_copy(1 - mx).start()
    y_copy(1 - mx).wait_recv()

    def pair_copy2(z):
        return remote(
            pair_out2.at[z], pair_in2.at[z], pair_send2.at[z], pair_recv2.at[z], ep=across
        )

    def col_copy2(z, slot):
        return remote(
            col_out2.at[z], col_in2.at[slot], col_send2.at[z], col_recv2.at[slot], ep=z * 2 + mx
        )

    for j in range(cols):
        z = (mz + 1 + j) % cols
        made = y_all[1 - mx, rep, z].astype(F32) + y_in[1 - mx, z].astype(F32)
        pair_out2[z] = made.astype(BF16)
        pair_copy2(z).start()
    y_copy(mx).wait_recv()
    for j in range(cols):
        z = (mz + 1 + j) % cols
        made = y_all[mx, rep, z].astype(F32) + y_in[mx, z].astype(F32)
        pair_copy2(z).wait_recv()
        mine = made + pair_in2[z].astype(F32)
        if j < cols - 1:
            col_out2[z] = mine.astype(BF16)
            col_copy2(z, mz).start()
        else:
            total[...] += mine
    for j in range(1, cols):
        z = (mz + j) % cols
        col_copy2(z, z).wait_recv()
        total[...] += col_in2[z].astype(F32)
    out_ref[...] = jnp.where(is_live, total[...], 0.0).astype(BF16)

    @pl.loop(1, owners)
    def _(i):
        to = (me + i) % owners
        remote(q_part(to), q_buf.at[me], q_send.at[to], q_recv.at[me], ep=to).wait_send()

    for x in range(2):
        y_copy(x).wait_send()
    for z in range(cols):
        pair_copy(z).wait_send()
        pair_copy2(z).wait_send()
    for j in range(1, cols):
        z = (mz + j) % cols
        col_copy(z, mz).wait_send()
        col_copy2(z, mz).wait_send()
        z_copy(z, me).wait_send()
    for j in range(cols):
        x_copy(((mz + j) % cols) * 2 + mx).wait_send()

    @pl.loop(0, owners)
    def _(e):
        s_copy(e, rep).wait_send()


def fast_local(
    owners,
    hidden_in,
    row_counts,
    qkv_new,
    cache_len,
    kv_cache,
    w_out,
    moe_gain,
    w_in,
    w_down,
    route_ids,
    route_weight,
):
    block, width = hidden_in.shape
    part = kv_cache.shape[-1]
    positions = kv_cache.shape[3]
    cols = owners // 2
    inner = w_down.shape[1]
    fresh = jnp.transpose(qkv_new, (1, 0, 2))
    w_planes = jnp.transpose(w_in.reshape(width, 2, inner), (1, 0, 2))
    vmem = pl.BlockSpec(memory_space=pltpu.VMEM)
    hbm = pl.BlockSpec(memory_space=pl.ANY)
    smem = pl.BlockSpec(memory_space=pltpu.SMEM)
    dma = pltpu.SemaphoreType.DMA
    wide = (cols, block, width)
    return pl.pallas_call(
        functools.partial(layer_kernel, owners),
        out_shape=jax.ShapeDtypeStruct((block, width), BF16),
        in_specs=[vmem, vmem, hbm, vmem, vmem, vmem, vmem, vmem, smem, hbm, hbm],
        out_specs=vmem,
        scratch_shapes=[
            pltpu.VMEM((2, 2, block, positions, part), BF16),
            pltpu.VMEM((owners, 3, block, part), BF16),
            pltpu.VMEM(wide, BF16),
            pltpu.VMEM(wide, BF16),
            pltpu.VMEM(wide, BF16),
            pltpu.VMEM(wide, BF16),
            pltpu.VMEM((block, width), F32),
            pltpu.VMEM((2, 2, cols, block, width + LANES), BF16),
            pltpu.VMEM((2, width, inner), BF16),
            pltpu.VMEM((inner, width), BF16),
            pltpu.VMEM((owners * block, inner), BF16),
            pltpu.VMEM((2, 2, cols, block, width), BF16),
            pltpu.VMEM((2, cols, block, width), BF16),
            pltpu.VMEM(wide, BF16),
            pltpu.VMEM(wide, BF16),
            pltpu.VMEM(wide, BF16),
            pltpu.VMEM(wide, BF16),
            dma((2,)),
            dma((2,)),
            dma((owners,)),
            dma((owners,)),
            dma((cols,)),
            dma((cols,)),
            dma((cols,)),
            dma((cols,)),
            dma((cols,)),
            dma((owners,)),
            dma((owners,)),
            dma((2, 2, cols)),
            dma((2,)),
            dma((2,)),
            dma((cols,)),
            dma((cols,)),
            dma((cols,)),
            dma((cols,)),
        ],
        compiler_params=pltpu.CompilerParams(
            collective_id=0, has_side_effects=True, vmem_limit_bytes=60 * 1024 * 1024
        ),
    )(
        fresh,
        cache_len,
        kv_cache,
        w_out,
        hidden_in,
        moe_gain.reshape(1, width),
        route_ids.T,
        route_weight.T,
        row_counts,
        w_planes,
        w_down.reshape(inner, width),
    )


def solution(mesh):
    placed = (
        P(("grp", "ep", "rep"), "seq"),
        P(("grp", "ep", "rep")),
        P(("grp", "ep", "rep"), None, None),
        P("grp", ("rep", "seq")),
        P(None, "grp", ("rep", "seq"), None, "ep"),
        P("ep", "seq"),
        P(),
        P(("ep", "rep"), None, None, "seq"),
        P(("ep", "rep"), "seq", None),
        P(("grp", "ep", "rep"), None),
        P(("grp", "ep", "rep"), None),
    )
    sizes = mesh.shape
    owners = sizes["ep"]
    one_step = sizes["seq"] == 1 and sizes["rep"] == 2 and owners % 2 == 0 and owners <= 8
    body = functools.partial(fast_local, owners) if one_step else local
    return jax.shard_map(
        body, mesh=mesh, in_specs=placed, out_specs=P(("grp", "ep", "rep"), "seq"), check_vma=False
    )
```

profile of v0, /device:TPU:0, one launch (start us, length us, event | category | flops | bytes accessed | tf_op | source)
XLA Modules:
  0.0 108.1 jit_solution(2749103540541598640)
XLA Ops:
  0.7 11.3 %copy.14 = bf16[1,2048,2,1408]{3,1,2,0:T(8,128)(2,1)} copy(bf16[1,2048,2,1408]{3,2,1,0:T(2,128)(2,1)} %param.18) | data formatting | bytes 23068672 | tf_op args[7]
  11.9 94.6 %shard_map.109 = bf16[32,2048]{1,0:T(8,128)(2,1)} custom-call(bf16[3,32,2048]{2,1,0:T(8,128)(2,1)} %bitcast.12, s32[8,32]{1,0:T(8,128)} %lens_ref.1, bf16[2,8,32,128,256]{4,3,2,1,0:T(8,128)(2,1)} %kv_hbm.1, bf16[256,2048]{1,0:T(8,128)(2,1)} %w_out_ref.1, bf16[32,2048]{1,0:T(8,128)(2,1)} %hidden_ref.1, f32[1,2048]{1,0:T(1,128)} %bitcast.13, ...), custom_call_target="tpu_custom_call" | custom-call | tf_op jit(solution)/shard_map/pallas_call | solution.py:530
  106.5 1.6 %copy.17 = bf16[32,2048]{1,0:T(8,128)(2,1)} copy(bf16[32,2048]{1,0:T(8,128)(2,1)} %shard_map.109) | data formatting | bytes 262144
where the time goes:
time: 109 us; the launch traced here: 108 us
  Pallas kernels  94.6 us (87%)
  local copies, waits for them, and re-layouts  12.8 us (12%)
    pallas_call x1, Pallas kernels, fast_local(): pl.pallas_call(functools.partial(layer_kernel, owners), out_shape=jax.Sha...  94.6 us
    unnamed x2, local copies, waits for them, and re-layouts  12.8 us

commit v1 on v0

--- a/solution.py
+++ b/solution.py
@@ -160,24 +160,25 @@
     col_in,
     total,
     rows_all,
+    w_raw,
     w_in_buf,
     w_down_buf,
     hidden_buf,
     y_all,
     y_in,
-    pair_out2,
-    pair_in2,
-    col_out2,
-    col_in2,
     kv_sem,
+    raw_sem,
     w_sem,
     q_send,
     q_recv,
+    f_send,
+    f_recv,
     pair_send,
     pair_recv,
     col_send,
     col_recv,
-    z_send,
+    up_send,
+    down_send,
     x_send,
     s_send,
     g_recv,
@@ -197,8 +198,10 @@
     block, width = hidden_ref.shape
     part = kv_buf.shape[-1]
     positions = kv_buf.shape[-2]
+    slots = kv_buf.shape[0]
     heads = part // HEAD_DIM
     used = heads * block
+    steps = owners
 
     def remote(src, dst, send, recv, ep=None, core=None):
         return pltpu.make_async_remote_copy(
@@ -210,19 +213,30 @@
             device_id_type=pl.DeviceIdType.MESH,
         )
 
-    def kv_copy(owner, slot):
-        return pltpu.make_async_copy(kv_hbm.at[:, owner], kv_buf.at[slot], kv_sem.at[slot])
-
-    def owner_of(j, s):
-        z = (mz + 1 + j) % cols
-        return z * 2 + (1 - mx if s == 0 else mx)
-
-    in_copy = pltpu.make_async_copy(w_in_hbm, w_in_buf, w_sem.at[0])
-    down_copy = pltpu.make_async_copy(w_down_hbm, w_down_buf, w_sem.at[1])
-    kv_copy(owner_of(0, 0), 0).start()
-    kv_copy(owner_of(0, 1), 1).start()
-    in_copy.start()
-    down_copy.start()
+    def z_of(j):
+        if cols == 4:
+            k = 3 - j
+            return (mz // 2 + k // 2) % 2 * 2 + (mz + k) % 2
+        return (mz + 1 + j) % cols
+
+    def owner_of(s):
+        return z_of(s % cols) * 2 + (1 - mx + s // cols) % 2
+
+    def kv_copy(s):
+        return pltpu.make_async_copy(
+            kv_hbm.at[:, owner_of(s)], kv_buf.at[s % slots], kv_sem.at[s % slots]
+        )
+
+    tiles = w_raw.shape[0]
+
+    def raw_copy(n):
+        return pltpu.make_async_copy(
+            w_in_hbm.at[:, :, pl.ds(n * LANES, LANES)], w_raw.at[n], raw_sem.at[n]
+        )
+
+    down_copy = pltpu.make_async_copy(w_down_hbm, w_down_buf, w_sem)
+    for s in range(slots):
+        kv_copy(s).start()
 
     barrier = pltpu.get_barrier_semaphore()
     for i in range(1, owners):
@@ -237,15 +251,33 @@
     )
     pl.semaphore_wait(barrier, owners)
 
-    def q_part(owner):
-        return qkv_ref.at[:, :, pl.ds(pl.multiple_of(owner * part, part), part)]
-
-    @pl.loop(1, owners)
-    def _(i):
-        to = (me + owners - i) % owners
-        remote(q_part(to), q_buf.at[me], q_send.at[to], q_recv.at[me], ep=to).start()
-
-    q_buf[me] = qkv_ref[:, :, pl.ds(pl.multiple_of(me * part, part), part)]
+    def lanes_of(owner):
+        return pl.ds(pl.multiple_of(owner * part, part), part)
+
+    def q_copy(to, slot):
+        return remote(
+            qkv_ref.at[pl.ds(0, 1), :, lanes_of(to)],
+            q_buf.at[slot, pl.ds(0, 1)],
+            q_send.at[to],
+            q_recv.at[slot],
+            ep=to,
+        )
+
+    def f_copy(to, slot):
+        return remote(
+            qkv_ref.at[pl.ds(1, 2), :, lanes_of(to)],
+            q_buf.at[slot, pl.ds(1, 2)],
+            f_send.at[to],
+            f_recv.at[slot],
+            ep=to,
+        )
+
+    for s in range(steps - 1):
+        q_copy(owner_of(s), me).start()
+    for s in range(steps - 1):
+        f_copy(owner_of(s), me).start()
+
+    q_buf[me] = qkv_ref[:, :, lanes_of(me)]
 
     is_live = lax.broadcasted_iota(jnp.int32, (block, 1), 0) < count_ref[0]
     expert_id = lax.broadcasted_iota(jnp.int32, (LANES, LANES), 0)
@@ -265,10 +297,15 @@
     scale = 1.0 / math.sqrt(HEAD_DIM)
     group = 8
 
-    def partial(owner, slot):
+    def partial(s):
+        owner, slot = owner_of(s), s % slots
+
+        @pl.when(owner != me)
+        def _():
+            q_copy(owner, owner).wait_recv()
+
+        kv_copy(s).wait()
         query = q_buf[owner, 0]
-        fresh_k = q_buf[owner, 1]
-        fresh_v = q_buf[owner, 2].astype(F32)
         zero = jnp.zeros_like(query)
         stack = [jnp.where(head_of == h, query, zero) for h in range(heads)]
         stack += [zero] * (LANES // block - heads)
@@ -287,6 +324,13 @@
         scores = lax.fori_loop(
             0, block // group, score_step, jnp.zeros((positions, LANES), F32)
         )
+
+        @pl.when(owner != me)
+        def _():
+            f_copy(owner, owner).wait_recv()
+
+        fresh_k = q_buf[owner, 1]
+        fresh_v = q_buf[owner, 2].astype(F32)
         fresh = lax.dot_general(fresh_k, queries, nt, preferred_element_type=F32)
         diag = lax.broadcasted_iota(jnp.int32, (block, LANES), 0) == (
             lax.broadcasted_iota(jnp.int32, (block, LANES), 1) % block
@@ -315,6 +359,11 @@
             return acc + jnp.dot(wide, values, preferred_element_type=F32)
 
         summed = lax.fori_loop(0, block // group, value_step, jnp.zeros((used, part), F32))
+
+        @pl.when(s + slots < steps)
+        def _():
+            kv_copy(s + slots).start()
+
         pieces = []
         for h in range(heads):
             rows = slice(h * block, (h + 1) * block)
@@ -323,11 +372,6 @@
         attended = jnp.concatenate(pieces, axis=1).astype(BF16)
         return jnp.dot(attended, w_out_ref[...], preferred_element_type=F32)
 
-    def arrive_q(owner):
-        @pl.when(owner != me)
-        def _():
-            remote(q_part(owner), q_buf.at[owner], q_send.at[owner], q_recv.at[owner], ep=owner).wait_recv()
-
     def pair_copy(z):
         return remote(pair_out.at[z], pair_in.at[z], pair_send.at[z], pair_recv.at[z], ep=across)
 
@@ -338,25 +382,18 @@
 
     @pl.loop(0, cols)
     def _(j):
-        z = (mz + 1 + j) % cols
-        first, second = owner_of(j, 0), owner_of(j, 1)
-        arrive_q(first)
-        kv_copy(first, 0).wait()
-        pair_out[z] = partial(first, 0).astype(BF16)
+        z = z_of(j)
+        pair_out[z] = partial(j).astype(BF16)
         pair_copy(z).start()
 
-        @pl.when(j < cols - 1)
-        def _():
-            kv_copy(owner_of(j + 1, 0), 0).start()
-
-        arrive_q(second)
-        kv_copy(second, 1).wait()
-        mine = partial(second, 1)
-
-        @pl.when(j < cols - 1)
-        def _():
-            kv_copy(owner_of(j + 1, 1), 1).start()
-
+    for n in range(tiles):
+        raw_copy(n).start()
+    down_copy.start()
+
+    @pl.loop(0, cols)
+    def _(j):
+        z = z_of(j)
+        mine = partial(cols + j)
         pair_copy(z).wait_recv()
         mine = mine + pair_in[z].astype(F32)
 
@@ -369,8 +406,43 @@
         def _():
             total[...] = mine
 
-    for j in range(1, cols):
-        z = (mz + j) % cols
+    flat = w_raw.reshape(tiles, 2 * width, LANES)
+    chunk = 2 * LANES
+    pick_row = lax.broadcasted_iota(jnp.int32, (chunk, chunk), 0)
+    pick_col = lax.broadcasted_iota(jnp.int32, (chunk, chunk), 1)
+    pick = jnp.where(
+        pick_col == pick_row % LANES * 2 + pick_row // LANES, 1.0, 0.0
+    ).astype(BF16)
+    turns = 2 * width // chunk
+    unroll = 4
+
+    def planes(low, high):
+        @pl.loop(low, high)
+        def _(turn):
+            for n in range(0, tiles, 2):
+                many = min(2, tiles - n)
+                for k in range(unroll):
+                    i = turn * unroll + k
+                    raw_rows = pl.ds(pl.multiple_of(i * chunk, chunk), chunk)
+                    out_rows = pl.ds(pl.multiple_of(i * LANES, LANES), LANES)
+                    both = jnp.concatenate(
+                        [flat[n + t, raw_rows, :] for t in range(many)], axis=1
+                    )
+                    split = jnp.dot(pick, both, preferred_element_type=F32).astype(BF16)
+                    for t in range(many):
+                        at = (n + t) * chunk
+                        lanes = slice(t * LANES, (t + 1) * LANES)
+                        w_in_buf[out_rows, at : at + LANES] = split[:LANES, lanes]
+                        w_in_buf[out_rows, at + LANES : at + chunk] = split[LANES:, lanes]
+
+    rounds = turns // unroll
+    cuts = [rounds * i // 4 for i in range(5)]
+    for n in range(tiles):
+        raw_copy(n).wait()
+    planes(cuts[0], cuts[1])
+
+    for j in range(cols - 1):
+        z = z_of(j)
         col_copy(z, z).wait_recv()
         total[...] += col_in[z].astype(F32)
     residual = (hidden_ref[...].astype(F32) + total[...]).astype(BF16)
@@ -383,8 +455,11 @@
         at = rows_all.at[e % 2, side, e // 2]
         return remote(at, at, send, g_recv.at[e % 2, side, e // 2], ep=ep, core=core)
 
-    def z_copy(z, e):
-        return row_copy(e, rep, z_send.at[z], ep=z * 2 + mx)
+    def up_copy(z):
+        return row_copy(z * 2 + mx, rep, up_send.at[z], ep=me + 2)
+
+    def lower_copy(z):
+        return row_copy(z * 2 + mx, rep, down_send.at[z], ep=me - 2)
 
     def x_copy(e):
         return row_copy(e, rep, x_send.at[e], ep=across)
@@ -392,24 +467,60 @@
     def s_copy(e, side):
         return row_copy(e, side, s_send.at[e], core=sister)
 
-    def y_copy(x):
-        return remote(y_all.at[x, sister], y_in.at[x], y_send.at[x], y_recv.at[x], core=sister)
+    def send_up(z):
+        @pl.when(mz < cols - 1)
+        def _():
+            up_copy(z).start()
+
+    def send_down(z):
+        @pl.when(mz > 0)
+        def _():
+            lower_copy(z).start()
+
+    send_up(mz)
+    send_down(mz)
+    x_copy(me).start()
+    s_copy(me, rep).start()
+    for d in range(1, cols):
+        planes(cuts[min(d, 4)], cuts[min(d + 1, 4)])
+
+        @pl.when(mz - d >= 0)
+        def _():
+            z = mz - d
+            x_copy(z * 2 + mx).wait_recv()
+            send_up(z)
+            x_copy(z * 2 + mx).start()
+            s_copy(z * 2 + mx, rep).start()
+
+        @pl.when(mz + d < cols)
+        def _():
+            z = mz + d
+            x_copy(z * 2 + mx).wait_recv()
+            send_down(z)
+            x_copy(z * 2 + mx).start()
+            s_copy(z * 2 + mx, rep).start()
+
+    for d in range(cols, 4):
+        planes(cuts[d], cuts[d + 1])
 
     expert = me * 2 + rep
-    tiles = w_in_buf.shape[2] // LANES
     half = owners * block
     step = 2 * LANES
 
-    def experts(x):
-        @pl.loop(0, tiles)
+    def gate_up(x, low, high):
+        @pl.loop(low, high)
         def _(n):
             rows = rows_all[x, :, :, :, :width].reshape(half, width)
             lanes = pl.ds(pl.multiple_of(n * LANES, LANES), LANES)
-            both_w = jnp.concatenate([w_in_buf[0, :, lanes], w_in_buf[1, :, lanes]], axis=1)
-            both = jnp.dot(rows, both_w, preferred_element_type=F32)
+            both = jnp.dot(
+                rows,
+                w_in_buf[:, pl.ds(pl.multiple_of(n * chunk, chunk), chunk)],
+                preferred_element_type=F32,
+            )
             gate, up = both[:, :LANES], both[:, LANES:]
-            hidden_buf[:, lanes] = (gate / (1.0 + jnp.exp(-gate)) * up).astype(BF16)
-
+            hidden_buf[x, :, lanes] = (gate / (1.0 + jnp.exp(-gate)) * up).astype(BF16)
+
+    def down(x):
         coefs = rows_all[x, :, :, :, width:].reshape(half, LANES).astype(F32)
         lane = lax.broadcasted_iota(jnp.int32, (half, LANES), 1)
         factor = jnp.sum(jnp.where(lane == expert, coefs, 0.0), axis=1, keepdims=True)
@@ -417,87 +528,108 @@
         @pl.loop(0, width // step)
         def _(n):
             lanes = pl.ds(pl.multiple_of(n * step, step), step)
-            made = jnp.dot(hidden_buf[...], w_down_buf[:, lanes], preferred_element_type=F32)
+            made = jnp.dot(hidden_buf[x], w_down_buf[:, lanes], preferred_element_type=F32)
             made = made.astype(BF16).astype(F32) * factor
             y_all[x, :, :, :, lanes] = made.astype(BF16).reshape(2, cols, block, step)
 
-    for j in range(1, cols):
-        z_copy((mz + j) % cols, me).start()
-    x_copy(me).start()
-    s_copy(me, rep).start()
-    for j in range(1, cols):
-        e = ((mz + j) % cols) * 2 + mx
-        z_copy(e // 2, e).wait_recv()
-        x_copy(e).start()
-        s_copy(e, rep).start()
-    in_copy.wait()
+    def y_copy(x, z):
+        return remote(
+            y_all.at[x, sister, z], y_in.at[x, z], y_send.at[x, z], y_recv.at[x, z], core=sister
+        )
+
+    def across_arrive(d):
+        @pl.when(mz - d >= 0)
+        def _():
+            e = (mz - d) * 2 + 1 - mx
+            x_copy(e).wait_recv()
+            s_copy(e, rep).start()
+
+        if d:
+
+            @pl.when(mz + d < cols)
+            def _():
+                e = (mz + d) * 2 + 1 - mx
+                x_copy(e).wait_recv()
+                s_copy(e, rep).start()
+
+    for z in range(cols):
+        s_copy(z * 2 + mx, sister).wait_recv()
+    gate_up(mx, 0, tiles // 2)
+    for d in range(cols - 1):
+        across_arrive(d)
+    gate_up(mx, tiles // 2, tiles)
+    across_arrive(cols - 1)
     down_copy.wait()
     for z in range(cols):
-        s_copy(z * 2 + mx, sister).wait_recv()
-    experts(mx)
-    y_copy(mx).start()
+        s_copy(z * 2 + 1 - mx, sister).wait_recv()
+    gate_up(1 - mx, 0, tiles)
+    down(1 - mx)
     for j in range(cols):
-        e = ((mz + j) % cols) * 2 + 1 - mx
-        x_copy(e).wait_recv()
-        s_copy(e, rep).start()
-    for z in range(cols):
-        s_copy(z * 2 + 1 - mx, sister).wait_recv()
-    experts(1 - mx)
-    y_copy(1 - mx).start()
-    y_copy(1 - mx).wait_recv()
+        y_copy(1 - mx, z_of(j)).start()
 
     def pair_copy2(z):
         return remote(
-            pair_out2.at[z], pair_in2.at[z], pair_send2.at[z], pair_recv2.at[z], ep=across
+            pair_out.at[z], pair_in.at[z], pair_send2.at[z], pair_recv2.at[z], ep=across
         )
 
     def col_copy2(z, slot):
         return remote(
-            col_out2.at[z], col_in2.at[slot], col_send2.at[z], col_recv2.at[slot], ep=z * 2 + mx
-        )
-
+            col_out.at[z], col_in.at[slot], col_send2.at[z], col_recv2.at[slot], ep=z * 2 + mx
+        )
+
+    for z in range(cols):
+        pair_copy(z).wait_send()
+    for j in range(cols - 1):
+        col_copy(z_of(j), mz).wait_send()
     for j in range(cols):
-        z = (mz + 1 + j) % cols
+        z = z_of(j)
+        y_copy(1 - mx, z).wait_recv()
         made = y_all[1 - mx, rep, z].astype(F32) + y_in[1 - mx, z].astype(F32)
-        pair_out2[z] = made.astype(BF16)
+        pair_out[z] = made.astype(BF16)
         pair_copy2(z).start()
-    y_copy(mx).wait_recv()
+    down(mx)
     for j in range(cols):
-        z = (mz + 1 + j) % cols
+        y_copy(mx, z_of(j)).start()
+    for j in range(cols):
+        z = z_of(j)
+        y_copy(mx, z).wait_recv()
         made = y_all[mx, rep, z].astype(F32) + y_in[mx, z].astype(F32)
         pair_copy2(z).wait_recv()
-        mine = made + pair_in2[z].astype(F32)
+        mine = made + pair_in[z].astype(F32)
         if j < cols - 1:
-            col_out2[z] = mine.astype(BF16)
+            col_out[z] = mine.astype(BF16)
             col_copy2(z, mz).start()
         else:
             total[...] += mine
-    for j in range(1, cols):
-        z = (mz + j) % cols
+    for j in range(cols - 1):
+        z = z_of(j)
         col_copy2(z, z).wait_recv()
-        total[...] += col_in2[z].astype(F32)
+        total[...] += col_in[z].astype(F32)
     out_ref[...] = jnp.where(is_live, total[...], 0.0).astype(BF16)
 
-    @pl.loop(1, owners)
-    def _(i):
-        to = (me + i) % owners
-        remote(q_part(to), q_buf.at[me], q_send.at[to], q_recv.at[me], ep=to).wait_send()
-
+    for s in range(steps - 1):
+        q_copy(owner_of(s), me).wait_send()
+        f_copy(owner_of(s), me).wait_send()
     for x in range(2):
-        y_copy(x).wait_send()
+        for z in range(cols):
+            y_copy(x, z).wait_send()
     for z in range(cols):
-        pair_copy(z).wait_send()
         pair_copy2(z).wait_send()
-    for j in range(1, cols):
-        z = (mz + j) % cols
-        col_copy(z, mz).wait_send()
-        col_copy2(z, mz).wait_send()
-        z_copy(z, me).wait_send()
-    for j in range(cols):
-        x_copy(((mz + j) % cols) * 2 + mx).wait_send()
-
-    @pl.loop(0, owners)
-    def _(e):
+        x_copy(z * 2 + mx).wait_send()
+    for j in range(cols - 1):
+        col_copy2(z_of(j), mz).wait_send()
+
+    for z in range(cols):
+
+        @pl.when((z <= mz) & (mz < cols - 1))
+        def _():
+            up_copy(z).wait_send()
+
+        @pl.when((z >= mz) & (mz > 0))
+        def _():
+            lower_copy(z).wait_send()
+
+    for e in range(owners):
         s_copy(e, rep).wait_send()
 
 
@@ -520,20 +652,21 @@
     positions = kv_cache.shape[3]
     cols = owners // 2
     inner = w_down.shape[1]
+    tiles = inner // LANES
     fresh = jnp.transpose(qkv_new, (1, 0, 2))
-    w_planes = jnp.transpose(w_in.reshape(width, 2, inner), (1, 0, 2))
     vmem = pl.BlockSpec(memory_space=pltpu.VMEM)
     hbm = pl.BlockSpec(memory_space=pl.ANY)
     smem = pl.BlockSpec(memory_space=pltpu.SMEM)
     dma = pltpu.SemaphoreType.DMA
     wide = (cols, block, width)
+    slots = min(3, owners)
     return pl.pallas_call(
         functools.partial(layer_kernel, owners),
         out_shape=jax.ShapeDtypeStruct((block, width), BF16),
         in_specs=[vmem, vmem, hbm, vmem, vmem, vmem, vmem, vmem, smem, hbm, hbm],
         out_specs=vmem,
         scratch_shapes=[
-            pltpu.VMEM((2, 2, block, positions, part), BF16),
+            pltpu.VMEM((slots, 2, block, positions, part), BF16),
             pltpu.VMEM((owners, 3, block, part), BF16),
             pltpu.VMEM(wide, BF16),
             pltpu.VMEM(wide, BF16),
@@ -541,19 +674,20 @@
             pltpu.VMEM(wide, BF16),
             pltpu.VMEM((block, width), F32),
             pltpu.VMEM((2, 2, cols, block, width + LANES), BF16),
-            pltpu.VMEM((2, width, inner), BF16),
+            pltpu.VMEM((tiles, width, 2, LANES), BF16),
+            pltpu.VMEM((width, 2 * inner), BF16),
             pltpu.VMEM((inner, width), BF16),
-            pltpu.VMEM((owners * block, inner), BF16),
+            pltpu.VMEM((2, owners * block, inner), BF16),
             pltpu.VMEM((2, 2, cols, block, width), BF16),
             pltpu.VMEM((2, cols, block, width), BF16),
-            pltpu.VMEM(wide, BF16),
-            pltpu.VMEM(wide, BF16),
-            pltpu.VMEM(wide, BF16),
-            pltpu.VMEM(wide, BF16),
-            dma((2,)),
-            dma((2,)),
+            dma((slots,)),
+            dma((tiles,)),
+            dma,
             dma((owners,)),
             dma((owners,)),
+            dma((owners,)),
+            dma((owners,)),
+            dma((cols,)),
             dma((cols,)),
             dma((cols,)),
             dma((cols,)),
@@ -562,15 +696,15 @@
             dma((owners,)),
             dma((owners,)),
             dma((2, 2, cols)),
-            dma((2,)),
-            dma((2,)),
+            dma((2, cols)),
+            dma((2, cols)),
             dma((cols,)),
             dma((cols,)),
             dma((cols,)),
             dma((cols,)),
         ],
         compiler_params=pltpu.CompilerParams(
-            collective_id=0, has_side_effects=True, vmem_limit_bytes=60 * 1024 * 1024
+            collective_id=0, has_side_effects=True, vmem_limit_bytes=63 * 1024 * 1024
         ),
     )(
         fresh,
@@ -582,7 +716,7 @@
         route_ids.T,
         route_weight.T,
         row_counts,
-        w_planes,
+        w_in.reshape(width, 2, inner),
         w_down.reshape(inner, width),
     )
 

time: 109 us -> 88 us (0.81)
  local copies, waits for them, and re-layouts: 12.8 us -> 1.57 us
  Pallas kernels: 94.6 us -> 85.6 us
    unnamed x2 -> x1, local copies, waits for them, and re-layouts: 12.8 us -> 1.57 us
    pallas_call x1, Pallas kernels: 94.6 us -> 85.6 us  [fast_local(): pl.pallas_call(functools.partial(layer_kernel, owners), out_shape=jax.Sha...]
where the time goes in v1:
time: 88 us; the launch traced here: 87.8 us
  Pallas kernels  85.6 us (97%)
  local copies, waits for them, and re-layouts  1.57 us (2%)
    pallas_call x1, Pallas kernels, fast_local(): pl.pallas_call(functools.partial(layer_kernel, owners), out_shape=jax.Sha...  85.6 us

profile of v1, /device:TPU:0, one launch (start us, length us, event | category | flops | bytes accessed | tf_op | source)
XLA Modules:
  0.0 87.8 jit_solution(5163866197452882460)
XLA Ops:
  0.7 85.6 %shard_map.109 = bf16[32,2048]{1,0:T(8,128)(2,1)} custom-call(bf16[3,32,2048]{2,1,0:T(8,128)(2,1)} %bitcast.8, s32[8,32]{1,0:T(8,128)} %lens_ref.1, bf16[2,8,32,128,256]{4,3,2,1,0:T(8,128)(2,1)} %kv_hbm.1, bf16[256,2048]{1,0:T(8,128)(2,1)} %w_out_ref.1, bf16[32,2048]{1,0:T(8,128)(2,1)} %hidden_ref.1, f32[1,2048]{1,0:T(1,128)} %bitcast.9, s32[6,32]{1,0:T(8,128)} %bitcast.10, ...), custom_call_target="tpu_custom_call" | custom-call | tf_op jit(solution)/shard_map/pallas_call | solution.py:663
  86.2 1.6 %copy.14 = bf16[32,2048]{1,0:T(8,128)(2,1)} copy(bf16[32,2048]{1,0:T(8,128)(2,1)} %shard_map.109) | data formatting | bytes 262144

commit v2 on v1

--- a/solution.py
+++ b/solution.py
@@ -154,6 +154,8 @@
     out_ref,
     kv_buf,
     q_buf,
+    own_out,
+    own_in,
     pair_out,
     pair_in,
     col_out,
@@ -171,8 +173,10 @@
     w_sem,
     q_send,
     q_recv,
-    f_send,
-    f_recv,
+    v_send,
+    v_recv,
+    own_send,
+    own_recv,
     pair_send,
     pair_recv,
     col_send,
@@ -219,8 +223,15 @@
             return (mz // 2 + k // 2) % 2 * 2 + (mz + k) % 2
         return (mz + 1 + j) % cols
 
+    def second(s):
+        t = (s + steps - 1) % steps
+        return (1 - t % 2) * ((t + steps - 1) // steps) + t // (steps - 1)
+
+    def turn_of(s):
+        return ((s + steps - 1) % steps + 1) // 2 - second(s)
+
     def owner_of(s):
-        return z_of(s % cols) * 2 + (1 - mx + s // cols) % 2
+        return z_of(turn_of(s)) * 2 + (1 - mx + second(s)) % 2
 
     def kv_copy(s):
         return pltpu.make_async_copy(
@@ -263,148 +274,50 @@
             ep=to,
         )
 
-    def f_copy(to, slot):
+    def v_copy(to, slot):
         return remote(
-            qkv_ref.at[pl.ds(1, 2), :, lanes_of(to)],
-            q_buf.at[slot, pl.ds(1, 2)],
-            f_send.at[to],
-            f_recv.at[slot],
+            qkv_ref.at[pl.ds(2, 1), :, lanes_of(to)],
+            q_buf.at[slot, pl.ds(1, 1)],
+            v_send.at[to],
+            v_recv.at[slot],
             ep=to,
         )
 
-    for s in range(steps - 1):
+    def own_copy(to, slot):
+        return remote(
+            own_out.at[to], own_in.at[slot], own_send.at[to], own_recv.at[slot], ep=to
+        )
+
+    for s in range(1, steps):
         q_copy(owner_of(s), me).start()
-    for s in range(steps - 1):
-        f_copy(owner_of(s), me).start()
-
-    q_buf[me] = qkv_ref[:, :, lanes_of(me)]
-
-    is_live = lax.broadcasted_iota(jnp.int32, (block, 1), 0) < count_ref[0]
-    expert_id = lax.broadcasted_iota(jnp.int32, (LANES, LANES), 0)
-    gates = gate_ref[...].astype(F32)
-    ids = jnp.concatenate([ids_ref[...]] * (LANES // block), axis=1)
-    gates = jnp.concatenate([gates] * (LANES // block), axis=1)
-    coef = jnp.zeros((LANES, LANES), F32)
-    for k in range(TOPK):
-        coef += jnp.where(expert_id == ids[k : k + 1], gates[k : k + 1], 0.0)
-    coef = coef.T[:block]
-    rows_all[mx, rep, mz, :, width:] = jnp.where(is_live, coef, 0.0).astype(BF16)
-
-    lane_row = lax.broadcasted_iota(jnp.int32, (1, LANES), 1) % block
-    pos_of = lax.broadcasted_iota(jnp.int32, (positions, LANES), 0)
+    for s in range(1, steps):
+        v_copy(owner_of(s), me).start()
+
     head_of = lax.broadcasted_iota(jnp.int32, (block, part), 1) // HEAD_DIM
-    row_mod = lax.broadcasted_iota(jnp.int32, (used, positions), 0) % block
     scale = 1.0 / math.sqrt(HEAD_DIM)
-    group = 8
-
-    def partial(s):
-        owner, slot = owner_of(s), s % slots
-
-        @pl.when(owner != me)
-        def _():
-            q_copy(owner, owner).wait_recv()
-
-        kv_copy(s).wait()
-        query = q_buf[owner, 0]
+    nt = (((1,), (1,)), ((), ()))
+    diag = lax.broadcasted_iota(jnp.int32, (block, LANES), 0) == (
+        lax.broadcasted_iota(jnp.int32, (block, LANES), 1) % block
+    )
+
+    def stacked(query):
         zero = jnp.zeros_like(query)
         stack = [jnp.where(head_of == h, query, zero) for h in range(heads)]
         stack += [zero] * (LANES // block - heads)
-        queries = jnp.concatenate(stack, axis=0)
-        nt = (((1,), (1,)), ((), ()))
-
-        def score_step(g, acc):
-            keys = kv_buf[slot, 0, pl.ds(g * group, group)].reshape(group * positions, part)
-            got = lax.dot_general(keys, queries, nt, preferred_element_type=F32)
-            for r in range(group):
-                acc = jnp.where(
-                    lane_row == g * group + r, got[r * positions : (r + 1) * positions], acc
-                )
-            return acc
-
-        scores = lax.fori_loop(
-            0, block // group, score_step, jnp.zeros((positions, LANES), F32)
-        )
-
-        @pl.when(owner != me)
-        def _():
-            f_copy(owner, owner).wait_recv()
-
-        fresh_k = q_buf[owner, 1]
-        fresh_v = q_buf[owner, 2].astype(F32)
-        fresh = lax.dot_general(fresh_k, queries, nt, preferred_element_type=F32)
-        diag = lax.broadcasted_iota(jnp.int32, (block, LANES), 0) == (
-            lax.broadcasted_iota(jnp.int32, (block, LANES), 1) % block
+        return jnp.concatenate(stack, axis=0)
+
+    for i in range(owners):
+        lanes = slice(i * part, (i + 1) * part)
+        fresh = lax.dot_general(
+            qkv_ref[1, :, lanes], stacked(qkv_ref[0, :, lanes]), nt, preferred_element_type=F32
         )
         own = jnp.sum(jnp.where(diag, fresh, 0.0), axis=0, keepdims=True) * scale
-        lens = jnp.concatenate([lens_ref[pl.ds(owner, 1), :]] * (LANES // block), axis=1)
-        in_cache = pos_of < lens
-        scores = jnp.where(in_cache, scores * scale, masked_score)
-        top = jnp.maximum(jnp.max(scores, axis=0, keepdims=True), own)
-        weights = jnp.where(in_cache, jnp.exp(scores - top), 0.0)
-        own_w = jnp.exp(own - top)
-        den = jnp.sum(weights, axis=0, keepdims=True) + own_w
-        own_t = jnp.broadcast_to(own_w, (LANES, LANES)).T
-        den_t = jnp.broadcast_to(den, (LANES, LANES)).T
-        weights_t = weights.T[:used]
-
-        def value_step(g, acc):
-            wide = jnp.concatenate(
-                [
-                    jnp.where(row_mod == g * group + r, weights_t, 0.0).astype(BF16)
-                    for r in range(group)
-                ],
-                axis=1,
-            )
-            values = kv_buf[slot, 1, pl.ds(g * group, group)].reshape(group * positions, part)
-            return acc + jnp.dot(wide, values, preferred_element_type=F32)
-
-        summed = lax.fori_loop(0, block // group, value_step, jnp.zeros((used, part), F32))
-
-        @pl.when(s + slots < steps)
-        def _():
-            kv_copy(s + slots).start()
-
-        pieces = []
-        for h in range(heads):
-            rows = slice(h * block, (h + 1) * block)
-            lanes = slice(h * HEAD_DIM, (h + 1) * HEAD_DIM)
-            pieces.append((summed[rows, lanes] + own_t[rows] * fresh_v[:, lanes]) / den_t[rows])
-        attended = jnp.concatenate(pieces, axis=1).astype(BF16)
-        return jnp.dot(attended, w_out_ref[...], preferred_element_type=F32)
-
-    def pair_copy(z):
-        return remote(pair_out.at[z], pair_in.at[z], pair_send.at[z], pair_recv.at[z], ep=across)
-
-    def col_copy(z, slot):
-        return remote(
-            col_out.at[z], col_in.at[slot], col_send.at[z], col_recv.at[slot], ep=z * 2 + mx
-        )
-
-    @pl.loop(0, cols)
-    def _(j):
-        z = z_of(j)
-        pair_out[z] = partial(j).astype(BF16)
-        pair_copy(z).start()
-
-    for n in range(tiles):
-        raw_copy(n).start()
-    down_copy.start()
-
-    @pl.loop(0, cols)
-    def _(j):
-        z = z_of(j)
-        mine = partial(cols + j)
-        pair_copy(z).wait_recv()
-        mine = mine + pair_in[z].astype(F32)
-
-        @pl.when(j < cols - 1)
-        def _():
-            col_out[z] = mine.astype(BF16)
-            col_copy(z, mz).start()
-
-        @pl.when(j == cols - 1)
-        def _():
-            total[...] = mine
+        own_out[i] = jnp.broadcast_to(own, own_out.shape[1:])
+    for s in range(1, steps):
+        own_copy(owner_of(s), me).start()
+    own_in[me] = own_out[me]
+    q_buf[me, 0] = qkv_ref[0, :, lanes_of(me)]
+    q_buf[me, 1] = qkv_ref[2, :, lanes_of(me)]
 
     flat = w_raw.reshape(tiles, 2 * width, LANES)
     chunk = 2 * LANES
@@ -436,10 +349,131 @@
                         w_in_buf[out_rows, at + LANES : at + chunk] = split[LANES:, lanes]
 
     rounds = turns // unroll
-    cuts = [rounds * i // 4 for i in range(5)]
+    first, early = 0, rounds // 2
+
+    is_live = lax.broadcasted_iota(jnp.int32, (block, 1), 0) < count_ref[0]
+    expert_id = lax.broadcasted_iota(jnp.int32, (LANES, LANES), 0)
+    gates = gate_ref[...].astype(F32)
+    ids = jnp.concatenate([ids_ref[...]] * (LANES // block), axis=1)
+    gates = jnp.concatenate([gates] * (LANES // block), axis=1)
+    coef = jnp.zeros((LANES, LANES), F32)
+    for k in range(TOPK):
+        coef += jnp.where(expert_id == ids[k : k + 1], gates[k : k + 1], 0.0)
+    coef = coef.T[:block]
+    rows_all[mx, rep, mz, :, width:] = jnp.where(is_live, coef, 0.0).astype(BF16)
+
+    lane_row = lax.broadcasted_iota(jnp.int32, (1, LANES), 1) % block
+    pos_of = lax.broadcasted_iota(jnp.int32, (positions, LANES), 0)
+    row_mod = lax.broadcasted_iota(jnp.int32, (used, positions), 0) % block
+    group = 8
+
+    def partial(s):
+        owner, slot = owner_of(s), s % slots
+
+        @pl.when(owner != me)
+        def _():
+            q_copy(owner, owner).wait_recv()
+
+        kv_copy(s).wait()
+        queries = stacked(q_buf[owner, 0])
+
+        scores = jnp.zeros((positions, LANES), F32)
+        for g in range(block // group):
+            keys = kv_buf[slot, 0, g * group : (g + 1) * group].reshape(group * positions, part)
+            got = lax.dot_general(keys, queries, nt, preferred_element_type=F32)
+            for r in range(group):
+                scores = jnp.where(
+                    lane_row == g * group + r, got[r * positions : (r + 1) * positions], scores
+                )
+
+        @pl.when(owner != me)
+        def _():
+            own_copy(owner, owner).wait_recv()
+
+        own = own_in[owner][:1]
+        lens = jnp.concatenate([lens_ref[pl.ds(owner, 1), :]] * (LANES // block), axis=1)
+        in_cache = pos_of < lens
+        scores = jnp.where(in_cache, scores * scale, masked_score)
+        top = jnp.maximum(jnp.max(scores, axis=0, keepdims=True), own)
+        weights = jnp.where(in_cache, jnp.exp(scores - top), 0.0)
+        own_w = jnp.exp(own - top)
+        den = jnp.sum(weights, axis=0, keepdims=True) + own_w
+        own_t = jnp.broadcast_to(own_w, (LANES, LANES)).T
+        den_t = jnp.broadcast_to(den, (LANES, LANES)).T
+        weights_t = weights.T[:used]
+
+        summed = jnp.zeros((used, part), F32)
+        for g in range(block // group):
+            wide = jnp.concatenate(
+                [
+                    jnp.where(row_mod == g * group + r, weights_t, 0.0).astype(BF16)
+                    for r in range(group)
+                ],
+                axis=1,
+            )
+            values = kv_buf[slot, 1, g * group : (g + 1) * group].reshape(group * positions, part)
+            summed += jnp.dot(wide, values, preferred_element_type=F32)
+
+        @pl.when(s + slots < steps)
+        def _():
+            kv_copy(s + slots).start()
+
+        @pl.when(owner != me)
+        def _():
+            v_copy(owner, owner).wait_recv()
+
+        fresh_v = q_buf[owner, 1].astype(F32)
+        pieces = []
+        for h in range(heads):
+            rows = slice(h * block, (h + 1) * block)
+            lanes = slice(h * HEAD_DIM, (h + 1) * HEAD_DIM)
+            pieces.append((summed[rows, lanes] + own_t[rows] * fresh_v[:, lanes]) / den_t[rows])
+        attended = jnp.concatenate(pieces, axis=1).astype(BF16)
+        return jnp.dot(attended, w_out_ref[...], preferred_element_type=F32)
+
+    def pair_copy(z):
+        return remote(pair_out.at[z], pair_in.at[z], pair_send.at[z], pair_recv.at[z], ep=across)
+
+    def col_copy(z, slot):
+        return remote(
+            col_out.at[z], col_in.at[slot], col_send.at[z], col_recv.at[slot], ep=z * 2 + mx
+        )
+
+    @pl.loop(0, steps)
+    def _(s):
+        j = turn_of(s)
+        z = z_of(j)
+        made = partial(s)
+
+        @pl.when(second(s) == 0)
+        def _():
+            pair_out[z] = made.astype(BF16)
+            pair_copy(z).start()
+
+        @pl.when(s == 1)
+        def _():
+            for n in range(tiles):
+                raw_copy(n).start()
+
+        @pl.when(s == steps - 1)
+        def _():
+            down_copy.start()
+
+        @pl.when((second(s) == 1) & (s > 0))
+        def _():
+            pair_copy(z).wait_recv()
+            col_out[z] = (made + pair_in[z].astype(F32)).astype(BF16)
+            col_copy(z, mz).start()
+
+        @pl.when(s == 0)
+        def _():
+            total[...] = made
+
     for n in range(tiles):
         raw_copy(n).wait()
-    planes(cuts[0], cuts[1])
+    planes(first, early)
+    pair_copy(mz).wait_recv()
+    total[...] += pair_in[mz].astype(F32)
 
     for j in range(cols - 1):
         z = z_of(j)
@@ -451,74 +485,88 @@
     inverse = lax.rsqrt(jnp.mean(wide * wide, axis=1, keepdims=True) + epsilon)
     rows_all[mx, rep, mz, :, :width] = (wide * inverse * gain_ref[...]).astype(BF16)
 
-    def row_copy(e, side, send, ep=None, core=None):
-        at = rows_all.at[e % 2, side, e // 2]
-        return remote(at, at, send, g_recv.at[e % 2, side, e // 2], ep=ep, core=core)
-
-    def up_copy(z):
-        return row_copy(z * 2 + mx, rep, up_send.at[z], ep=me + 2)
-
-    def lower_copy(z):
-        return row_copy(z * 2 + mx, rep, down_send.at[z], ep=me - 2)
-
-    def x_copy(e):
-        return row_copy(e, rep, x_send.at[e], ep=across)
-
-    def s_copy(e, side):
-        return row_copy(e, side, s_send.at[e], core=sister)
-
-    def send_up(z):
+    cut = g_recv.shape[-1]
+    bit = block // cut
+
+    def row_copy(e, side, h, send, ep=None, core=None):
+        at = rows_all.at[e % 2, side, e // 2, pl.ds(h * bit, bit)]
+        return remote(at, at, send, g_recv.at[e % 2, side, e // 2, h], ep=ep, core=core)
+
+    def up_copy(z, h):
+        return row_copy(z * 2 + mx, rep, h, up_send.at[z, h], ep=me + 2)
+
+    def lower_copy(z, h):
+        return row_copy(z * 2 + mx, rep, h, down_send.at[z, h], ep=me - 2)
+
+    def x_copy(e, h):
+        return row_copy(e, rep, h, x_send.at[e, h], ep=across)
+
+    def s_copy(e, side, h):
+        return row_copy(e, side, h, s_send.at[e, h], core=sister)
+
+    def send_up(z, h):
         @pl.when(mz < cols - 1)
         def _():
-            up_copy(z).start()
-
-    def send_down(z):
+            up_copy(z, h).start()
+
+    def send_down(z, h):
         @pl.when(mz > 0)
         def _():
-            lower_copy(z).start()
-
-    send_up(mz)
-    send_down(mz)
-    x_copy(me).start()
-    s_copy(me, rep).start()
+            lower_copy(z, h).start()
+
+    for h in range(cut):
+        send_up(mz, h)
+        send_down(mz, h)
+        x_copy(me, h).start()
+        s_copy(me, rep, h).start()
+    planes(early, rounds * 3 // 4)
     for d in range(1, cols):
-        planes(cuts[min(d, 4)], cuts[min(d + 1, 4)])
-
-        @pl.when(mz - d >= 0)
-        def _():
-            z = mz - d
-            x_copy(z * 2 + mx).wait_recv()
-            send_up(z)
-            x_copy(z * 2 + mx).start()
-            s_copy(z * 2 + mx, rep).start()
-
-        @pl.when(mz + d < cols)
-        def _():
-            z = mz + d
-            x_copy(z * 2 + mx).wait_recv()
-            send_down(z)
-            x_copy(z * 2 + mx).start()
-            s_copy(z * 2 + mx, rep).start()
-
-    for d in range(cols, 4):
-        planes(cuts[d], cuts[d + 1])
+        if d == min(2, cols - 1):
+            planes(rounds * 3 // 4, rounds)
+        for h in range(cut):
+
+            @pl.when(mz - d >= 0)
+            def _():
+                z = mz - d
+                x_copy(z * 2 + mx, h).wait_recv()
+                send_up(z, h)
+                x_copy(z * 2 + mx, h).start()
+                s_copy(z * 2 + mx, rep, h).start()
+
+            @pl.when(mz + d < cols)
+            def _():
+                z = mz + d
+                x_copy(z * 2 + mx, h).wait_recv()
+                send_down(z, h)
+                x_copy(z * 2 + mx, h).start()
+                s_copy(z * 2 + mx, rep, h).start()
 
     expert = me * 2 + rep
     half = owners * block
-    step = 2 * LANES
+    step = 4 * LANES
 
     def gate_up(x, low, high):
-        @pl.loop(low, high)
-        def _(n):
+        def some(at, many):
             rows = rows_all[x, :, :, :, :width].reshape(half, width)
-            lanes = pl.ds(pl.multiple_of(n * LANES, LANES), LANES)
             both = jnp.dot(
                 rows,
-                w_in_buf[:, pl.ds(pl.multiple_of(n * chunk, chunk), chunk)],
+                w_in_buf[:, pl.ds(pl.multiple_of(at * chunk, chunk), many * chunk)],
                 preferred_element_type=F32,
             )
-            gate, up = both[:, :LANES], both[:, LANES:]
-            hidden_buf[x, :, lanes] = (gate / (1.0 + jnp.exp(-gate)) * up).astype(BF16)
+            for t in range(many):
+                gate = both[:, t * chunk : t * chunk + LANES]
+                up = both[:, t * chunk + LANES : (t + 1) * chunk]
+                lanes = pl.ds(pl.multiple_of((at + t) * LANES, LANES), LANES)
+                hidden_buf[x, :, lanes] = (gate / (1.0 + jnp.exp(-gate)) * up).astype(BF16)
+
+        pairs = (high - low) // 2
+
+        @pl.loop(0, pairs)
+        def _(n):
+            some(low + 2 * n, 2)
+
+        if low + 2 * pairs < high:
+            some(high - 1, 1)
 
     def down(x):
         coefs = rows_all[x, :, :, :, width:].reshape(half, LANES).astype(F32)
@@ -538,30 +586,35 @@
         )
 
     def across_arrive(d):
-        @pl.when(mz - d >= 0)
-        def _():
-            e = (mz - d) * 2 + 1 - mx
-            x_copy(e).wait_recv()
-            s_copy(e, rep).start()
-
-        if d:
-
-            @pl.when(mz + d < cols)
+        for h in range(cut):
+
+            @pl.when(mz - d >= 0)
             def _():
-                e = (mz + d) * 2 + 1 - mx
-                x_copy(e).wait_recv()
-                s_copy(e, rep).start()
-
-    for z in range(cols):
-        s_copy(z * 2 + mx, sister).wait_recv()
-    gate_up(mx, 0, tiles // 2)
+                e = (mz - d) * 2 + 1 - mx
+                x_copy(e, h).wait_recv()
+                s_copy(e, rep, h).start()
+
+            if d:
+
+                @pl.when(mz + d < cols)
+                def _():
+                    e = (mz + d) * 2 + 1 - mx
+                    x_copy(e, h).wait_recv()
+                    s_copy(e, rep, h).start()
+
+    def sister_arrive(x):
+        for z in range(cols):
+            for h in range(cut):
+                s_copy(z * 2 + x, sister, h).wait_recv()
+
+    sister_arrive(mx)
+    gate_up(mx, 0, tiles // 4 * 2)
     for d in range(cols - 1):
         across_arrive(d)
-    gate_up(mx, tiles // 2, tiles)
+    gate_up(mx, tiles // 4 * 2, tiles)
     across_arrive(cols - 1)
     down_copy.wait()
-    for z in range(cols):
-        s_copy(z * 2 + 1 - mx, sister).wait_recv()
+    sister_arrive(1 - mx)
     gate_up(1 - mx, 0, tiles)
     down(1 - mx)
     for j in range(cols):
@@ -607,15 +660,17 @@
         total[...] += col_in[z].astype(F32)
     out_ref[...] = jnp.where(is_live, total[...], 0.0).astype(BF16)
 
-    for s in range(steps - 1):
+    for s in range(1, steps):
         q_copy(owner_of(s), me).wait_send()
-        f_copy(owner_of(s), me).wait_send()
+        v_copy(owner_of(s), me).wait_send()
+        own_copy(owner_of(s), me).wait_send()
     for x in range(2):
         for z in range(cols):
             y_copy(x, z).wait_send()
     for z in range(cols):
         pair_copy2(z).wait_send()
-        x_copy(z * 2 + mx).wait_send()
+        for h in range(cut):
+            x_copy(z * 2 + mx, h).wait_send()
     for j in range(cols - 1):
         col_copy2(z_of(j), mz).wait_send()
 
@@ -623,14 +678,17 @@
 
         @pl.when((z <= mz) & (mz < cols - 1))
         def _():
-            up_copy(z).wait_send()
+            for h in range(cut):
+                up_copy(z, h).wait_send()
 
         @pl.when((z >= mz) & (mz > 0))
         def _():
-            lower_copy(z).wait_send()
+            for h in range(cut):
+                lower_copy(z, h).wait_send()
 
     for e in range(owners):
-        s_copy(e, rep).wait_send()
+        for h in range(cut):
+            s_copy(e, rep, h).wait_send()
 
 
 def fast_local(
@@ -660,6 +718,7 @@
     dma = pltpu.SemaphoreType.DMA
     wide = (cols, block, width)
     slots = min(3, owners)
+    cut = 2
     return pl.pallas_call(
         functools.partial(layer_kernel, owners),
         out_shape=jax.ShapeDtypeStruct((block, width), BF16),
@@ -667,7 +726,9 @@
         out_specs=vmem,
         scratch_shapes=[
             pltpu.VMEM((slots, 2, block, positions, part), BF16),
-            pltpu.VMEM((owners, 3, block, part), BF16),
+            pltpu.VMEM((owners, 2, block, part), BF16),
+            pltpu.VMEM((owners, 8, LANES), F32),
+            pltpu.VMEM((owners, 8, LANES), F32),
             pltpu.VMEM(wide, BF16),
             pltpu.VMEM(wide, BF16),
             pltpu.VMEM(wide, BF16),
@@ -687,15 +748,17 @@
             dma((owners,)),
             dma((owners,)),
             dma((owners,)),
+            dma((owners,)),
+            dma((owners,)),
             dma((cols,)),
             dma((cols,)),
             dma((cols,)),
             dma((cols,)),
-            dma((cols,)),
-            dma((cols,)),
-            dma((owners,)),
-            dma((owners,)),
-            dma((2, 2, cols)),
+            dma((cols, cut)),
+            dma((cols, cut)),
+            dma((owners, cut)),
+            dma((owners, cut)),
+            dma((2, 2, cols, cut)),
             dma((2, cols)),
             dma((2, cols)),
             dma((cols,)),
@@ -737,7 +800,7 @@
     )
     sizes = mesh.shape
     owners = sizes["ep"]
-    one_step = sizes["seq"] == 1 and sizes["rep"] == 2 and owners % 2 == 0 and owners <= 8
+    one_step = sizes["seq"] == 1 and sizes["rep"] == 2 and owners in (4, 8)
     body = functools.partial(fast_local, owners) if one_step else local
     return jax.shard_map(
         body, mesh=mesh, in_specs=placed, out_specs=P(("grp", "ep", "rep"), "seq"), check_vma=False

time: 88 us -> 78.9 us (0.90)
  Pallas kernels: 85.6 us -> 76.5 us
    pallas_call x1, Pallas kernels: 85.6 us -> 76.5 us  [fast_local(): pl.pallas_call(functools.partial(layer_kernel, owners), out_shape=jax.Sha...]
where the time goes in v2:
time: 78.9 us; the launch traced here: 78.7 us
  Pallas kernels  76.5 us (97%)
  local copies, waits for them, and re-layouts  1.57 us (2%)
    pallas_call x1, Pallas kernels, fast_local(): pl.pallas_call(functools.partial(layer_kernel, owners), out_shape=jax.Sha...  76.5 us

profile of v2, /device:TPU:0, one launch (start us, length us, event | category | flops | bytes accessed | tf_op | source)
XLA Modules:
  0.0 78.7 jit_solution(4394981743850230403)
XLA Ops:
  0.7 76.5 %shard_map.109 = bf16[32,2048]{1,0:T(8,128)(2,1)} custom-call(bf16[3,32,2048]{2,1,0:T(8,128)(2,1)} %bitcast.8, s32[8,32]{1,0:T(8,128)} %lens_ref.1, bf16[2,8,32,128,256]{4,3,2,1,0:T(8,128)(2,1)} %kv_hbm.1, bf16[256,2048]{1,0:T(8,128)(2,1)} %w_out_ref.1, bf16[32,2048]{1,0:T(8,128)(2,1)} %hidden_ref.1, f32[1,2048]{1,0:T(1,128)} %bitcast.9, s32[6,32]{1,0:T(8,128)} %bitcast.10, ...), custom_call_target="tpu_custom_call" | custom-call | tf_op jit(solution)/shard_map/pallas_call | solution.py:722
  77.1 1.6 %copy.14 = bf16[32,2048]{1,0:T(8,128)(2,1)} copy(bf16[32,2048]{1,0:T(8,128)(2,1)} %shard_map.109) | data formatting | bytes 262144

commit v3 on v2

--- a/solution.py
+++ b/solution.py
@@ -568,21 +568,29 @@
         if low + 2 * pairs < high:
             some(high - 1, 1)
 
-    def down(x):
+    turns_down = width // step // 2
+    span = width // 2
+
+    def down(x, f):
         coefs = rows_all[x, :, :, :, width:].reshape(half, LANES).astype(F32)
         lane = lax.broadcasted_iota(jnp.int32, (half, LANES), 1)
         factor = jnp.sum(jnp.where(lane == expert, coefs, 0.0), axis=1, keepdims=True)
 
-        @pl.loop(0, width // step)
+        @pl.loop(f * turns_down, (f + 1) * turns_down)
         def _(n):
             lanes = pl.ds(pl.multiple_of(n * step, step), step)
             made = jnp.dot(hidden_buf[x], w_down_buf[:, lanes], preferred_element_type=F32)
             made = made.astype(BF16).astype(F32) * factor
             y_all[x, :, :, :, lanes] = made.astype(BF16).reshape(2, cols, block, step)
 
-    def y_copy(x, z):
+    def y_copy(x, z, f):
+        lanes = pl.ds(f * span, span)
         return remote(
-            y_all.at[x, sister, z], y_in.at[x, z], y_send.at[x, z], y_recv.at[x, z], core=sister
+            y_all.at[x, sister, z, :, lanes],
+            y_in.at[x, z, :, lanes],
+            y_send.at[x, z, f],
+            y_recv.at[x, z, f],
+            core=sister,
         )
 
     def across_arrive(d):
@@ -611,68 +619,89 @@
     gate_up(mx, 0, tiles // 4 * 2)
     for d in range(cols - 1):
         across_arrive(d)
-    gate_up(mx, tiles // 4 * 2, tiles)
+    gate_up(mx, tiles // 4 * 2, tiles // 4 * 4)
     across_arrive(cols - 1)
+    gate_up(mx, tiles // 4 * 4, tiles)
     down_copy.wait()
     sister_arrive(1 - mx)
     gate_up(1 - mx, 0, tiles)
-    down(1 - mx)
-    for j in range(cols):
-        y_copy(1 - mx, z_of(j)).start()
-
-    def pair_copy2(z):
+    for f in range(2):
+        down(1 - mx, f)
+        for j in range(cols):
+            y_copy(1 - mx, z_of(j), f).start()
+
+    def pair_copy2(z, f):
+        lanes = pl.ds(f * span, span)
         return remote(
-            pair_out.at[z], pair_in.at[z], pair_send2.at[z], pair_recv2.at[z], ep=across
-        )
-
-    def col_copy2(z, slot):
+            pair_out.at[z, :, lanes],
+            pair_in.at[z, :, lanes],
+            pair_send2.at[z, f],
+            pair_recv2.at[z, f],
+            ep=across,
+        )
+
+    def col_copy2(z, slot, f):
+        lanes = pl.ds(f * span, span)
         return remote(
-            col_out.at[z], col_in.at[slot], col_send2.at[z], col_recv2.at[slot], ep=z * 2 + mx
+            col_out.at[z, :, lanes],
+            col_in.at[slot, :, lanes],
+            col_send2.at[z, f],
+            col_recv2.at[slot, f],
+            ep=z * 2 + mx,
         )
 
     for z in range(cols):
         pair_copy(z).wait_send()
     for j in range(cols - 1):
         col_copy(z_of(j), mz).wait_send()
-    for j in range(cols):
-        z = z_of(j)
-        y_copy(1 - mx, z).wait_recv()
-        made = y_all[1 - mx, rep, z].astype(F32) + y_in[1 - mx, z].astype(F32)
-        pair_out[z] = made.astype(BF16)
-        pair_copy2(z).start()
-    down(mx)
-    for j in range(cols):
-        y_copy(mx, z_of(j)).start()
-    for j in range(cols):
-        z = z_of(j)
-        y_copy(mx, z).wait_recv()
-        made = y_all[mx, rep, z].astype(F32) + y_in[mx, z].astype(F32)
-        pair_copy2(z).wait_recv()
-        mine = made + pair_in[z].astype(F32)
-        if j < cols - 1:
-            col_out[z] = mine.astype(BF16)
-            col_copy2(z, mz).start()
-        else:
-            total[...] += mine
-    for j in range(cols - 1):
-        z = z_of(j)
-        col_copy2(z, z).wait_recv()
-        total[...] += col_in[z].astype(F32)
-    out_ref[...] = jnp.where(is_live, total[...], 0.0).astype(BF16)
+    for f in range(2):
+        lanes = slice(f * span, (f + 1) * span)
+        for j in range(cols):
+            z = z_of(j)
+            y_copy(1 - mx, z, f).wait_recv()
+            made = y_all[1 - mx, rep, z, :, lanes].astype(F32)
+            made += y_in[1 - mx, z, :, lanes].astype(F32)
+            pair_out[z, :, lanes] = made.astype(BF16)
+            pair_copy2(z, f).start()
+    for f in range(2):
+        down(mx, f)
+        for j in range(cols):
+            y_copy(mx, z_of(j), f).start()
+    for f in range(2):
+        lanes = slice(f * span, (f + 1) * span)
+        for j in range(cols):
+            z = z_of(j)
+            y_copy(mx, z, f).wait_recv()
+            made = y_all[mx, rep, z, :, lanes].astype(F32) + y_in[mx, z, :, lanes].astype(F32)
+            pair_copy2(z, f).wait_recv()
+            mine = made + pair_in[z, :, lanes].astype(F32)
+            if j < cols - 1:
+                col_out[z, :, lanes] = mine.astype(BF16)
+                col_copy2(z, mz, f).start()
+            else:
+                total[:, lanes] += mine
+    for f in range(2):
+        lanes = slice(f * span, (f + 1) * span)
+        for j in range(cols - 1):
+            z = z_of(j)
+            col_copy2(z, z, f).wait_recv()
+            total[:, lanes] += col_in[z, :, lanes].astype(F32)
+        out_ref[:, lanes] = jnp.where(is_live, total[:, lanes], 0.0).astype(BF16)
 
     for s in range(1, steps):
         q_copy(owner_of(s), me).wait_send()
         v_copy(owner_of(s), me).wait_send()
         own_copy(owner_of(s), me).wait_send()
-    for x in range(2):
+    for f in range(2):
         for z in range(cols):
-            y_copy(x, z).wait_send()
+            y_copy(0, z, f).wait_send()
+            y_copy(1, z, f).wait_send()
+            pair_copy2(z, f).wait_send()
+        for j in range(cols - 1):
+            col_copy2(z_of(j), mz, f).wait_send()
     for z in range(cols):
-        pair_copy2(z).wait_send()
         for h in range(cut):
             x_copy(z * 2 + mx, h).wait_send()
-    for j in range(cols - 1):
-        col_copy2(z_of(j), mz).wait_send()
 
     for z in range(cols):
 
@@ -759,12 +788,12 @@
             dma((owners, cut)),
             dma((owners, cut)),
             dma((2, 2, cols, cut)),
-            dma((2, cols)),
-            dma((2, cols)),
-            dma((cols,)),
-            dma((cols,)),
-            dma((cols,)),
-            dma((cols,)),
+            dma((2, cols, 2)),
+            dma((2, cols, 2)),
+            dma((cols, 2)),
+            dma((cols, 2)),
+            dma((cols, 2)),
+            dma((cols, 2)),
         ],
         compiler_params=pltpu.CompilerParams(
             collective_id=0, has_side_effects=True, vmem_limit_bytes=63 * 1024 * 1024

time: 78.9 us -> 77.4 us (0.981)
  Pallas kernels: 76.5 us -> 75 us
    pallas_call x1, Pallas kernels: 76.5 us -> 75 us  [fast_local(): pl.pallas_call(functools.partial(layer_kernel, owners), out_shape=jax.Sha...]
where the time goes in v3:
time: 77.4 us; the launch traced here: 77.2 us
  Pallas kernels  75 us (97%)
  local copies, waits for them, and re-layouts  1.57 us (2%)
    pallas_call x1, Pallas kernels, fast_local(): pl.pallas_call(functools.partial(layer_kernel, owners), out_shape=jax.Sha...  75 us
    unnamed x1, local copies, waits for them, and re-layouts  1.57 us

profile of v3, /device:TPU:0, one launch (start us, length us, event | category | flops | bytes accessed | tf_op | source)
XLA Modules:
  0.0 77.2 jit_solution(12635306753940377327)
XLA Ops:
  0.7 75.0 %shard_map.109 = bf16[32,2048]{1,0:T(8,128)(2,1)} custom-call(bf16[3,32,2048]{2,1,0:T(8,128)(2,1)} %bitcast.8, s32[8,32]{1,0:T(8,128)} %lens_ref.1, bf16[2,8,32,128,256]{4,3,2,1,0:T(8,128)(2,1)} %kv_hbm.1, bf16[256,2048]{1,0:T(8,128)(2,1)} %w_out_ref.1, bf16[32,2048]{1,0:T(8,128)(2,1)} %hidden_ref.1, f32[1,2048]{1,0:T(1,128)} %bitcast.9, s32[6,32]{1,0:T(8,128)} %bitcast.10, ...), custom_call_target="tpu_custom_call" | custom-call | tf_op jit(solution)/shard_map/pallas_call | solution.py:751
  75.6 1.6 %copy.14 = bf16[32,2048]{1,0:T(8,128)(2,1)} copy(bf16[32,2048]{1,0:T(8,128)(2,1)} %shard_map.109) | data formatting | bytes 262144
